TPU v7x, 256 devices: a whole 4x4x8 slice. The times are simulated.
256 devices in a mesh: outer: 8 (over z), inner: 32 (over y, x, core).
Axes of the slice: x: 4, y: 4, z: 8, core: 2. Of those that a mesh axis runs over, the one named last changes fastest.
Arguments:
- context: bfloat16 [32768, 4096], P(('outer', 'inner')), may hold values from -5 to 5
- query_acts: bfloat16 [64, 4096], replicated, may hold values from -5 to 5
- norm_gain: float32 [4096], replicated, may hold values from 0.25 to 1.75
- w_query: bfloat16 [4096, 2048], P('inner'), may hold values from -0.078125 to 0.078125
- w_key: bfloat16 [4096, 512], P('inner'), may hold values from -0.453125 to 0.453125
- value_weight: bfloat16 [4096, 512], P('inner'), may hold values from -0.09375 to 0.09375
- lengths: int32 [256], replicated, may hold values from 64 to 128, as said below
Outputs:
- block_out: bfloat16 [32768, 2048], P(('outer', 'inner'))
- query_out: bfloat16 [64, 2048], replicated
Inputs may be any that keep to these rules, and one draw needn't show every extreme that they name: `lengths`: valid tokens of a block are its first ones; the rest of it is padding.
All inputs are finite; a program needn't handle non-finite values.
Results may differ from a plain program's by a relative error of at most 0.004.
The roundings to bfloat16 on the way count: a program that leaves them out, or rounds other values in their place, can miss the bound.
Values may be sent and summed in bfloat16 or wider, within the bound.
No kernel may reach another device: no remote copies, remote signals or barrier semaphores. Data moves between devices by JAX's collectives and lax.ppermute only.
A program may use at most 320 MiB of HBM per device.

v0:
```python
import jax
import jax.numpy as jnp
from jax import lax
from jax.sharding import PartitionSpec as P

QUERY_HEADS = 16
KEY_VALUE_HEADS = 4
HEAD_SIZE = 128
epsilon = 1e-05


def broadcast(block, axis, owner):
    block = jnp.where(lax.axis_index(axis) == owner, block, jnp.zeros_like(block))
    return lax.psum(block, axis)


def normalize(matrix, norm_gain):
    widened = matrix.astype(jnp.float32)
    factor = lax.rsqrt(jnp.mean(widened * widened, axis=-1, keepdims=True) + epsilon)
    return (widened * factor * norm_gain).astype(jnp.bfloat16)


def attend_part(query_rows, key_row_block, value_matrix, allowed):
    count_of_rows = query_rows.shape[0]
    head_groups = query_rows.reshape(
        count_of_rows, KEY_VALUE_HEADS, QUERY_HEADS // KEY_VALUE_HEADS, HEAD_SIZE
    )
    per_head_keys = key_row_block.reshape(key_row_block.shape[0], KEY_VALUE_HEADS, HEAD_SIZE)
    per_head_values = value_matrix.reshape(value_matrix.shape[0], KEY_VALUE_HEADS, HEAD_SIZE)
    scores = jnp.einsum(
        "rhgd,khd->hgrk", head_groups, per_head_keys, preferred_element_type=jnp.float32
    ) * HEAD_SIZE ** (-0.5)
    scores = jnp.where(allowed, scores, -jnp.inf)
    maxima = jnp.max(scores, axis=-1)
    weights = jnp.exp(scores - maxima[..., None])
    sum_exp = jnp.sum(weights, axis=-1)
    numerator = jnp.einsum(
        "hgrk,khd->rhgd",
        weights.astype(jnp.bfloat16),
        per_head_values,
        preferred_element_type=jnp.float32,
    )
    return (
        maxima.reshape(QUERY_HEADS, count_of_rows),
        sum_exp.reshape(QUERY_HEADS, count_of_rows),
        numerator.reshape(count_of_rows, QUERY_HEADS * HEAD_SIZE),
    )


def spread(factor):
    return jnp.repeat(factor.T, HEAD_SIZE, axis=1)


def combine(former, latter):
    maxima = jnp.maximum(former[0], latter[0])
    scale_one = jnp.exp(former[0] - maxima)
    scale_two = jnp.exp(latter[0] - maxima)
    return (
        maxima,
        former[1] * scale_one + latter[1] * scale_two,
        former[2] * spread(scale_one) + latter[2] * spread(scale_two),
    )


def finish(pieces):
    return (pieces[2] / spread(pieces[1])).astype(jnp.bfloat16)


def share_anchor(stacked):
    return broadcast(stacked, ("outer", "inner"), 0)


def per_device(context, query_acts, norm_gain, w_query, w_key, value_weight, lengths):
    block_rows = context.shape[0]
    normed = jnp.concatenate(
        [normalize(context, norm_gain), normalize(query_acts, norm_gain)], axis=0
    )

    def apply_weight(whole_weight):
        return jnp.dot(normed, whole_weight, preferred_element_type=jnp.float32).astype(
            jnp.bfloat16
        )

    whole_q, whole_k, whole_v = (
        lax.all_gather(w_query, "inner", axis=0, tiled=True),
        lax.all_gather(w_key, "inner", axis=0, tiled=True),
        lax.all_gather(value_weight, "inner", axis=0, tiled=True),
    )
    projected_k = apply_weight(whole_k)
    projected_v = apply_weight(whole_v)
    anchor = share_anchor(jnp.stack([projected_k[:block_rows], projected_v[:block_rows]]))
    projected_q = apply_weight(whole_q)
    position = lax.axis_index(("outer", "inner"))
    own_length = lengths[position]
    anchor_length = lengths[0]
    places = jnp.arange(block_rows, dtype=jnp.int32)
    causal = places[:, None] >= places[None, :]
    block_q = projected_q[:block_rows]
    block_k = projected_k[:block_rows]
    block_v = projected_v[:block_rows]
    query_q = projected_q[block_rows:]
    query_k = projected_k[block_rows:]
    query_v = projected_v[block_rows:]
    query_count = query_q.shape[0]
    own_allowed = causal & (places[None, :] < own_length)
    anchor_allowed = jnp.broadcast_to(
        (places[None, :] < anchor_length) & (position > 0), (block_rows, block_rows)
    )
    allowed = jnp.concatenate([anchor_allowed, own_allowed], axis=1)
    key_row_block = jnp.concatenate([anchor[0], block_k], axis=0)
    value_rows = jnp.concatenate([anchor[1], block_v], axis=0)
    block_out = finish(attend_part(block_q, key_row_block, value_rows, allowed))
    reached = jnp.broadcast_to(places[None, :] < own_length, (query_count, block_rows))
    block_part = attend_part(query_q, block_k, block_v, reached)
    highest = lax.pmax(block_part[0], ("outer", "inner"))
    rescale = jnp.exp(block_part[0] - highest)
    summed_parts = lax.psum(
        (block_part[1] * rescale, block_part[2] * spread(rescale)), ("outer", "inner")
    )
    merged = (highest, summed_parts[0], summed_parts[1])
    query_places = jnp.arange(query_count, dtype=jnp.int32)
    self_part = attend_part(
        query_q, query_k, query_v, query_places[:, None] >= query_places[None, :]
    )
    return (block_out, finish(combine(merged, self_part)))


def solution(mesh):
    in_specs = (
        P(("outer", "inner"), None),
        P(),
        P(),
        P("inner", None),
        P("inner", None),
        P("inner", None),
        P(),
    )
    out_specs = (P(("outer", "inner"), None), P())
    return jax.shard_map(
        per_device, mesh=mesh, in_specs=in_specs, out_specs=out_specs, check_vma=False
    )
```

profile of v0, /device:TPU:2, one launch (start us, length us, event | category | flops | bytes accessed | tf_op | source)
XLA Modules:
  0.0 875.9 jit_solution(4082930749184454192)
XLA Ops:
  7.2 0.7 all-gather.4.cloned.1.call-update
  8.0 0.7 all-gather.6.cloned.1.call-update
  8.7 1.2 fusion.9
  10.0 1.5 fusion
  11.5 0.9 fusion.11
  12.5 0.3 fusion.2
  12.8 51.5 %all-gather.4.cloned.1.call-done = bf16[4096,512]{1,0:T(8,128)(2,1)} async-done(((bf16[128,512]{1,0:T(8,128)(2,1)}), bf16[4096,512]{1,0:T(8,128)(2,1)}) %all-gather.4.cloned.1.call-update) | async-done | bytes 4194320 | tf_op jit(solution)/shard_map/all_gather | solution.py:86
  64.3 3.2 convolution_convert_fusion.2
  67.6 49.9 %all-gather.6.cloned.1.call-done = bf16[4096,512]{1,0:T(8,128)(2,1)} async-done(((bf16[128,512]{1,0:T(8,128)(2,1)}), bf16[4096,512]{1,0:T(8,128)(2,1)}) %all-gather.6.cloned.1.call-update) | async-done | bytes 4194320 | tf_op jit(solution)/shard_map/all_gather | solution.py:87
  117.5 3.2 convolution_convert_fusion.1
  120.7 0.7 maximum_select_fusion
  121.5 0.5 all-gather.8.cloned.1.call-update
  122.1 0.6 fusion.52
  122.7 0.6 compare_and_fusion
  123.2 0.6 iota_compare_fusion.2
  124.1 0.8 copy.28
  124.9 0.7 concatenate.28
  125.6 0.6 reshape.106
  126.2 0.6 reshape.109
  126.9 246.7 %all-reduce.3.cloned.1.call-done = bf16[2,128,512]{2,1,0:T(8,128)(2,1)} async-done(((bf16[2,128,512]{2,1,0:T(8,128)(2,1)}), bf16[2,128,512]{2,1,0:T(8,128)(2,1)}) %all-reduce.3.cloned.1.call-update) | async-done | bytes 262160 | tf_op jit(solution)/shard_map/psum | solution.py:14
  373.5 1.0 fusion.49
  374.6 0.8 copy.56
  375.4 76.8 %all-gather.8.cloned.1.call-done = bf16[4096,2048]{1,0:T(8,128)(2,1)} async-done(((bf16[128,2048]{1,0:T(8,128)(2,1)}), bf16[4096,2048]{1,0:T(8,128)(2,1)}) %all-gather.8.cloned.1.call-update) | async-done | bytes 16777232 | tf_op jit(solution)/shard_map/all_gather | solution.py:85
  452.2 7.7 convolution_convert_fusion
  459.9 0.4 reshape.98
  460.3 0.5 fusion.53
  460.8 0.3 fusion.3
  461.2 0.5 fusion.12
  461.8 0.3 copy.34
  462.4 0.3 copy-done.9
  462.7 0.4 fusion.54
  463.1 76.0 %pmax.7 = f32[16,64]{1,0:T(8,128)S(1)} all-reduce(f32[16,64]{1,0:T(8,128)S(1)} %bitcast.97), channel_id=1, replica_groups=mesh['outer'=8,'inner'=32] {'outer','inner'}, use_global_device_ids=true, to_apply=%region_6.7 | all-reduce | flops 1024 | bytes 8192 | tf_op jit(solution)/shard_map/pmax | solution.py:115
  539.1 0.4 fusion.19
  539.5 74.4 %psum.23 = f32[16,64]{1,0:T(8,128)S(1)} all-reduce(f32[16,64]{1,0:T(8,128)S(1)} %get-tuple-element.13), channel_id=1, replica_groups=mesh['outer'=8,'inner'=32] {'outer','inner'}, use_global_device_ids=true, to_apply=%region_10.11 | all-reduce | flops 1024 | bytes 8192 | tf_op jit(solution)/shard_map/psum | solution.py:117
  614.0 0.4 fusion.55
  614.6 0.3 convolution_bitcast_fusion
  614.9 0.3 copy.45
  615.2 0.2 reshape.110
  615.5 0.3 convolution_bitcast_fusion.1
  615.8 0.3 copy.38
  616.2 0.2 reshape.103
  616.7 1.0 bitcast_multiply_fusion.2
  617.8 0.3 broadcast_in_dim.68
  618.2 1.2 fusion.14
  619.3 247.2 %all-reduce.5.cloned.1.call-done = f32[64,2048]{1,0:T(8,128)} async-done(((f32[64,2048]{1,0:T(8,128)}), f32[64,2048]{1,0:T(8,128)}) %all-reduce.5.cloned.1.call-update) | async-done | bytes 524304 | tf_op jit(solution)/shard_map/psum | solution.py:117
  866.7 0.2 broadcast_in_dim.75
  866.9 0.2 broadcast_in_dim.74
  867.1 2.2 fusion.16
  (58 shorter events, 2.0 us)
Async XLA Ops:
  7.2 4.4 copy-start.1
  7.2 5.3 copy-start
  7.2 5.3 copy-start.10
  7.2 57.1 %all-gather.4.cloned.1.call-start = ((), (), s32[]{:S(2)}) async-start(), calls=%async_computation | async-start | bytes 4325376 | tf_op jit(solution)/shard_map/all_gather | solution.py:86
  7.9 109.5 %all-gather.6.cloned.1.call-start = ((), (), s32[]{:S(2)}) async-start(), calls=%async_computation.1 | async-start | bytes 4325376 | tf_op jit(solution)/shard_map/all_gather | solution.py:87
  8.7 364.9 %all-reduce.3.cloned.1.call-start = ((), (), s32[]{:S(2)}) async-start(), calls=%async_computation.2 | async-start | bytes 524288 | tf_op jit(solution)/shard_map/psum | solution.py:14
  12.5 105.0 %copy-start.3 = (bf16[64,4096]{1,0:T(8,128)(2,1)}, bf16[64,4096]{1,0:T(8,128)(2,1)S(1)}, u32[]{:S(2)}) copy-start(bf16[64,4096]{1,0:T(8,128)(2,1)S(1)} %fusion.11) | copy-start | bytes 1572868
  67.6 54.5 %copy-start.11 = (s32[256]{0:T(256)S(1)}, s32[256]{0:T(256)}, u32[]{:S(2)}) copy-start(s32[256]{0:T(256)} %param.13) | copy-start | bytes 3076
  120.6 331.5 %copy-start.4 = (bf16[64,4096]{1,0:T(8,128)(2,1)S(1)}, bf16[64,4096]{1,0:T(8,128)(2,1)}, u32[]{:S(2)}) copy-start(bf16[64,4096]{1,0:T(8,128)(2,1)} %copy-done.3) | copy-start | bytes 1572868
  121.4 330.7 %all-gather.8.cloned.1.call-start = ((), (), s32[]{:S(2)}) async-start(), calls=%async_computation.3 | async-start | bytes 17301504 | tf_op jit(solution)/shard_map/all_gather | solution.py:85
  122.0 744.5 %all-reduce.5.cloned.1.call-start = ((), (), s32[]{:S(2)}) async-start(), calls=%async_computation.4 | async-start | bytes 1048576 | tf_op jit(solution)/shard_map/psum | solution.py:117
  459.8 0.9 copy-start.2
  460.3 0.9 copy-start.5
  460.3 1.0 copy-start.6
  461.2 1.0 slice-start
  461.7 0.9 copy-start.9
  461.8 152.2 %copy-start.8 = (bf16[64,4,128]{2,1,0:T(4,128)(2,1)S(1)}, bf16[64,4,128]{2,1,0:T(4,128)(2,1)}, u32[]{:S(2)}) copy-start(bf16[64,4,128]{2,1,0:T(4,128)(2,1)} %reshape.106) | copy-start | bytes 196612
  462.1 152.5 %copy-start.7 = (bf16[64,4,128]{2,1,0:T(4,128)(2,1)S(1)}, bf16[64,4,128]{2,1,0:T(4,128)(2,1)}, u32[]{:S(2)}) copy-start(bf16[64,4,128]{2,1,0:T(4,128)(2,1)} %reshape.109) | copy-start | bytes 196612
Sparse Core Ops, SparseCore 0:
  10.6 53.7 all-gather.3
  66.9 50.5 all-gather.5
  123.5 250.0 all-reduce.2
  375.9 76.1 all-gather.7
  617.9 248.6 all-reduce.4
where the time goes:
time: 876 us
  waiting for transfers between devices  674 us (77%)
  blocking collectives  150 us (17%)
  matrix products  16.3 us (2%)
  between operations  14.2 us (2%)
  other arithmetic  11.4 us (1%)
  local copies, waits for them, and re-layouts  9.33 us (1%)
    psum x1, waiting for transfers between devices, per_device(): lax.psum((block_part[1] * rescale, block_part[2] * spread(rescale)), ('ou...  247 us
    psum x1, waiting for transfers between devices, broadcast(): return lax.psum(block, axis)  247 us
    all_gather x1, waiting for transfers between devices, per_device(): lax.all_gather(w_query, 'inner', axis=0, tiled=True)  76.8 us
    pmax x1, blocking collectives, per_device(): highest = lax.pmax(block_part[0], ('outer', 'inner'))  76 us
    psum x1, blocking collectives, per_device(): lax.psum((block_part[1] * rescale, block_part[2] * spread(rescale)), ('ou...  74.4 us
    all_gather x1, waiting for transfers between devices, per_device(): lax.all_gather(w_key, 'inner', axis=0, tiled=True)  51.5 us
    all_gather x1, waiting for transfers between devices, per_device(): lax.all_gather(value_weight, 'inner', axis=0, tiled=True)  49.9 us
  transfers between devices with their start and end apart: 5, of which 5 were waited for; matrix products, arithmetic and copies ran while one was open for 2% of the time, Pallas kernels for 0%

commit v1 on v0

--- a/solution.py
+++ b/solution.py
@@ -11,7 +11,7 @@
 
 def broadcast(block, axis, owner):
     block = jnp.where(lax.axis_index(axis) == owner, block, jnp.zeros_like(block))
-    return lax.psum(block, axis)
+    return jnp.sum(jax.lax.all_gather(block, axis), 0)
 
 
 def normalize(matrix, norm_gain):

time: 876 us -> 782 us (0.89)
  waiting for transfers between devices: 674 us -> 560 us
  other arithmetic: 11.4 us -> 32.1 us
    psum x1 -> x0, waiting for transfers between devices: 247 us -> none  [broadcast(): return lax.psum(block, axis)]
    all_gather x0 -> x1, waiting for transfers between devices: none -> 212 us  [broadcast(): return jnp.sum(jax.lax.all_gather(block, axis), 0)]
    psum x1, waiting for transfers between devices: 247 us -> 171 us  [per_device(): lax.psum((block_part[1] * rescale, block_part[2] * spread(rescale)), ('ou...]
    reduce_sum x0 -> x1, other arithmetic: none -> 21.3 us  [broadcast(): return jnp.sum(jax.lax.all_gather(block, axis), 0)]
where the time goes in v1:
time: 782 us; the launch traced here: 780 us
  waiting for transfers between devices  560 us (72%)
  blocking collectives  151 us (19%)
  other arithmetic  32.1 us (4%)
  matrix products  16.5 us (2%)
  between operations  14.2 us (2%)
    all_gather x1, waiting for transfers between devices, broadcast(): return jnp.sum(jax.lax.all_gather(block, axis), 0)  212 us
    psum x1, waiting for transfers between devices, per_device(): lax.psum((block_part[1] * rescale, block_part[2] * spread(rescale)), ('ou...  171 us
    all_gather x1, waiting for transfers between devices, per_device(): lax.all_gather(w_query, 'inner', axis=0, tiled=True)  76.4 us
    pmax x1, blocking collectives, per_device(): highest = lax.pmax(block_part[0], ('outer', 'inner'))  76 us
    psum x1, blocking collectives, per_device(): lax.psum((block_part[1] * rescale, block_part[2] * spread(rescale)), ('ou...  75.2 us
    all_gather x1, waiting for transfers between devices, per_device(): lax.all_gather(w_key, 'inner', axis=0, tiled=True)  49.5 us
    all_gather x1, waiting for transfers between devices, per_device(): lax.all_gather(value_weight, 'inner', axis=0, tiled=True)  49.2 us
    reduce_sum x1, other arithmetic, broadcast(): return jnp.sum(jax.lax.all_gather(block, axis), 0)  21.3 us
  transfers between devices with their start and end apart: 5, of which 5 were waited for; matrix products, arithmetic and copies ran while one was open for 2% of the time, Pallas kernels for 0%

profile of v1, /device:TPU:2, one launch (start us, length us, event | category | flops | bytes accessed | tf_op | source)
XLA Modules:
  0.0 780.3 jit_solution(13975303522686498026)
XLA Ops:
  7.2 0.7 all-gather.5.cloned.1.call-update
  8.0 0.7 all-gather.7.cloned.1.call-update
  8.7 0.7 all-gather.11.cloned.1.call-update
  9.5 1.3 fusion.52
  10.8 0.6 iota_compare_fusion.2
  11.5 1.2 fusion.9
  12.7 1.5 fusion
  14.3 0.2 fusion.11
  14.5 0.3 fusion.2
  14.8 49.5 %all-gather.5.cloned.1.call-done = bf16[4096,512]{1,0:T(8,128)(2,1)} async-done(((bf16[128,512]{1,0:T(8,128)(2,1)}), bf16[4096,512]{1,0:T(8,128)(2,1)}) %all-gather.5.cloned.1.call-update) | async-done | bytes 4194320 | tf_op jit(solution)/shard_map/all_gather | solution.py:86
  64.3 3.2 convolution_convert_fusion.2
  67.5 0.7 copy-done.5
  68.3 49.2 %all-gather.7.cloned.1.call-done = bf16[4096,512]{1,0:T(8,128)(2,1)} async-done(((bf16[128,512]{1,0:T(8,128)(2,1)}), bf16[4096,512]{1,0:T(8,128)(2,1)}) %all-gather.7.cloned.1.call-update) | async-done | bytes 4194320 | tf_op jit(solution)/shard_map/all_gather | solution.py:87
  117.4 3.3 convolution_convert_fusion.1
  120.9 76.4 %all-gather.11.cloned.1.call-done = bf16[4096,2048]{1,0:T(8,128)(2,1)} async-done(((bf16[128,2048]{1,0:T(8,128)(2,1)}), bf16[4096,2048]{1,0:T(8,128)(2,1)}) %all-gather.11.cloned.1.call-update) | async-done | bytes 16777232 | tf_op jit(solution)/shard_map/all_gather | solution.py:85
  197.3 7.7 convolution_convert_fusion
  205.0 0.2 reshape.133
  205.2 0.4 fusion.54
  205.6 0.4 fusion.19
  206.0 76.0 %pmax.7 = f32[16,64]{1,0:T(8,128)S(1)} all-reduce(f32[16,64]{1,0:T(8,128)S(1)} %bitcast.99), channel_id=1, replica_groups=mesh['outer'=8,'inner'=32] {'outer','inner'}, use_global_device_ids=true, to_apply=%region_6.7 | all-reduce | flops 1024 | bytes 8192 | tf_op jit(solution)/shard_map/pmax | solution.py:115
  282.1 0.3 convolution_bitcast_fusion.1
  282.4 0.3 copy.57
  282.8 0.2 reshape.134
  283.0 0.2 broadcast_in_dim.71
  283.2 1.0 bitcast_multiply_fusion.2
  284.3 0.8 maximum_select_fusion
  285.1 0.6 compare_and_fusion
  285.9 0.1 copy.46
  286.2 75.2 %psum.15 = f32[16,64]{1,0:T(8,128)S(1)} all-reduce(f32[16,64]{1,0:T(8,128)S(1)} %get-tuple-element.13), channel_id=1, replica_groups=mesh['outer'=8,'inner'=32] {'outer','inner'}, use_global_device_ids=true, to_apply=%region_10.11 | all-reduce | flops 1024 | bytes 8192 | tf_op jit(solution)/shard_map/psum | solution.py:117
  361.4 0.4 fusion.55
  362.2 0.3 convolution_bitcast_fusion
  362.5 0.3 copy.64
  362.9 0.2 reshape.141
  363.1 0.4 reshape.129
  363.4 170.7 %all-reduce.2.cloned.1.call-done = f32[64,2048]{1,0:T(8,128)} async-done(((f32[64,2048]{1,0:T(8,128)}), f32[64,2048]{1,0:T(8,128)}) %all-reduce.2.cloned.1.call-update) | async-done | bytes 524304 | tf_op jit(solution)/shard_map/psum | solution.py:117
  534.2 0.2 broadcast_in_dim.74
  534.4 0.2 broadcast_in_dim.75
  534.6 0.2 broadcast_in_dim.76
  534.8 2.2 fusion.16
  537.0 211.8 %all-gather.9.cloned.1.call-done = bf16[256,2,128,512]{3,2,1,0:T(8,128)(2,1)} async-done(((bf16[1,2,128,512]{3,2,1,0:T(8,128)(2,1)}), bf16[256,2,128,512]{3,2,1,0:T(8,128)(2,1)}) %all-gather.9.cloned.1.call-update) | async-done | bytes 67108880 | tf_op jit(solution)/shard_map/all_gather | solution.py:14
  748.8 21.3 %reduce_sum.59 = bf16[2,128,512]{2,1,0:T(8,128)(2,1)S(1)} reduce(bf16[256,2,128,512]{3,2,1,0:T(8,128)(2,1)} %all-gather.9.cloned.1.call-done, bf16[]{:T(256)} %constant.10.clone.1), dimensions={0}, to_apply=%region_2.3 | reduce | flops 33423360 | bytes 67371008 | tf_op jit(solution)/shard_map/reduce_sum | solution.py:14
  770.3 0.1 copy.48
  770.4 0.5 fusion.53
  770.9 0.3 fusion.3
  771.4 0.5 fusion.12
  771.9 0.3 copy.53
  772.3 0.3 broadcast_in_dim.68
  772.6 1.2 fusion.14
  (53 shorter events, 1.5 us)
Async XLA Ops:
  7.2 7.1 copy-start.1
  7.2 7.3 copy-start
  7.2 7.1 copy-start.7
  7.2 57.1 %all-gather.5.cloned.1.call-start = ((), (), s32[]{:S(2)}) async-start(), calls=%async_computation | async-start | bytes 4325376 | tf_op jit(solution)/shard_map/all_gather | solution.py:86
  7.9 109.5 %all-gather.7.cloned.1.call-start = ((), (), s32[]{:S(2)}) async-start(), calls=%async_computation.1 | async-start | bytes 4325376 | tf_op jit(solution)/shard_map/all_gather | solution.py:87
  8.7 188.6 %all-gather.11.cloned.1.call-start = ((), (), s32[]{:S(2)}) async-start(), calls=%async_computation.3 | async-start | bytes 17301504 | tf_op jit(solution)/shard_map/all_gather | solution.py:85
  9.4 524.7 %all-reduce.2.cloned.1.call-start = ((), (), s32[]{:S(2)}) async-start(), calls=%async_computation.4 | async-start | bytes 1048576 | tf_op jit(solution)/shard_map/psum | solution.py:117
  14.5 49.9 %copy-start.3 = (bf16[64,4096]{1,0:T(8,128)(2,1)}, bf16[64,4096]{1,0:T(8,128)(2,1)S(1)}, u32[]{:S(2)}) copy-start(bf16[64,4096]{1,0:T(8,128)(2,1)S(1)} %fusion.11) | copy-start | bytes 1572868
  67.5 0.7 copy-start.5
  68.3 129.0 %copy-start.4 = (bf16[64,4096]{1,0:T(8,128)(2,1)S(1)}, bf16[64,4096]{1,0:T(8,128)(2,1)}, u32[]{:S(2)}) copy-start(bf16[64,4096]{1,0:T(8,128)(2,1)} %copy-done.3) | copy-start | bytes 1572868
  120.8 76.5 %copy-start.6 = (bf16[192,512]{1,0:T(8,128)(2,1)}, bf16[192,512]{1,0:T(8,128)(2,1)S(1)}, u32[]{:S(2)}) copy-start(bf16[192,512]{1,0:T(8,128)(2,1)S(1)} %convolution_convert_fusion.1) | copy-start | bytes 589828
  205.0 81.2 %copy-start.2 = (bf16[192,2048]{1,0:T(8,128)(2,1)}, bf16[192,2048]{1,0:T(8,128)(2,1)S(1)}, u32[]{:S(2)}) copy-start(bf16[192,2048]{1,0:T(8,128)(2,1)S(1)} %convolution_convert_fusion) | copy-start | bytes 2359300
  283.0 3.1 slice-start.1
  283.0 3.1 slice-start.2
  284.3 464.5 %all-gather.9.cloned.1.call-start = ((), (), s32[]{:S(2)}) async-start(), calls=%async_computation.2 | async-start | bytes 67371008 | tf_op jit(solution)/shard_map/all_gather | solution.py:14
  361.8 1.2 slice-start
Sparse Core Ops, SparseCore 0:
  10.6 53.7 all-gather.4
  66.9 50.5 all-gather.6
  120.0 77.2 all-gather.10
  284.4 249.7 all-reduce.1
  537.6 211.1 all-gather.8
